TPU v7x, 1024 devices: a whole 8x8x8 slice. The times are simulated.
1024 devices in a mesh: hi: 32 (over z_lo, y), lo: 32 (over x, z_hi, core).
Axes of the slice: x: 8, y: 8, z: 8 (z_hi: 2, z_lo: 4; z = z_hi * 4 + z_lo), core: 2. Of those that a mesh axis runs over, the one named last changes fastest.
Arguments:
- amplitudes: float32 [2, 1024, 512, 256], P(None, ('hi', 'lo')), may hold values from -6 to 6
- joined_gates: float32 [2, 2, 512, 512], replicated, may hold values from -0.1875 to 0.1875
- pair_gates: float32 [2, 2, 2, 2], replicated, may hold values from -3 to 3
- global_angles: float32 [2, 1024], P(None, ('hi', 'lo')), may hold values from -3.140625 to 3.140625
- local_phases: float32 [2, 17], replicated, may hold values from -3.140625 to 3.140625
- slice_bits: int32 [17], replicated, may hold values from 0 to 1
- coupled_qubits: int32 [2, 17], replicated, may hold values from 0 to 16
- gate_layout: int32 [9], replicated, may hold values from 0 to 8, each once
Outputs:
- evolved: float32 [2, 1024, 512, 256], P(None, ('hi', 'lo'))
Inputs may be any that keep to these rules, and one draw needn't show every extreme that they name: `gate_layout`: each of 0 to 8 once.
All inputs are finite; a program needn't handle non-finite values.
Results may differ from a plain program's by a relative error of at most 0.0001.
Values sent between devices are 32-bit elements; how exact they have to be, the bound alone decides.
A program may use at most 32 MiB of HBM per device.

v0:
```python
import math

import jax
import jax.numpy as jnp
from jax import lax
from jax.sharding import PartitionSpec as P

ROW_BITS = 9
COL_BITS = 8
LAYERS = 2
ROWS = 512
COLS = 256
LQ = 17


def partner_2(value, axis, bit):
    mask = 2**bit
    pairs = [(source, source ^ mask) for source in range(lax.axis_size(axis))]
    return lax.ppermute(value, axis, pairs)


def bit_angles(angles, bit_count, length):
    positions = jnp.arange(length, dtype=jnp.int32)
    summed = jnp.zeros((length,), jnp.float32)
    for bit_pos in range(bit_count):
        chosen = (positions >> bit_pos & 1).astype(jnp.float32)
        summed = summed + chosen * angles[bit_pos]
    return summed


def qubit_angles(local_phases, slice_bits, coupled_qubits, layer_id):
    qubits = jnp.arange(LQ, dtype=jnp.int32)
    matches = (coupled_qubits[layer_id][:, None] == qubits[None, :]).astype(jnp.float32)
    flipped = jnp.sum(matches * slice_bits[:, None].astype(jnp.float32), axis=0)
    return local_phases[layer_id] + math.pi * flipped


def folded_gate(joined_gates, layer_id, device_angle, row_angles):
    turned = row_angles + device_angle
    cosine = jnp.cos(turned)[None, :]
    sine = jnp.sin(turned)[None, :]
    gate_real = joined_gates[layer_id, 0]
    gate_imag = joined_gates[layer_id, 1]
    return (gate_real * cosine - gate_imag * sine, gate_real * sine + gate_imag * cosine)


def row_order(gate_layout):
    positions = jnp.arange(ROWS, dtype=jnp.int32)
    source = jnp.zeros((ROWS,), jnp.int32)
    for bit_pos in range(ROW_BITS):
        place = jnp.left_shift(jnp.ones((), jnp.int32), gate_layout[bit_pos])
        source = source + (positions >> bit_pos & 1) * place
    return source


def stacked_product(weight_real, weight_imag, block_real, block_imag):
    weights = jnp.concatenate([weight_real, weight_imag], axis=0)
    col_total = block_real.shape[1]
    row_total = weight_real.shape[0]
    inputs = jnp.concatenate([block_real, block_imag], axis=1)
    product = jnp.dot(
        weights, inputs, precision=lax.Precision.HIGHEST, preferred_element_type=jnp.float32
    )
    new_real = product[:row_total, :col_total] - product[row_total:, col_total:]
    new_imag = product[:row_total, col_total:] + product[row_total:, :col_total]
    return (new_real, new_imag)


def column_phase(new_real, new_imag, col_angles):
    cosine = jnp.cos(col_angles)[None, :]
    sine = jnp.sin(col_angles)[None, :]
    turned = jnp.stack([new_real * cosine - new_imag * sine, new_real * sine + new_imag * cosine])
    return turned[:, None]


def combine(self_real, self_imag, first, cross_real, cross_imag, second):
    new_real = (
        self_real * first[0]
        - self_imag * first[1]
        + cross_real * second[0]
        - cross_imag * second[1]
    )
    new_imag = (
        self_real * first[1]
        + self_imag * first[0]
        + cross_real * second[1]
        + cross_imag * second[0]
    )
    return jnp.stack([new_real, new_imag])


def pair_update(block, pair_gates, layer_id, bit_pos):
    own_bit = lax.axis_index("lo") >> bit_pos & 1
    other_bit = 1 - own_bit
    coeff_real = pair_gates[layer_id, 0]
    coeff_imag = pair_gates[layer_id, 1]
    partner = partner_2(block, "lo", bit_pos)
    return combine(
        coeff_real[own_bit, own_bit],
        coeff_imag[own_bit, own_bit],
        block,
        coeff_real[own_bit, other_bit],
        coeff_imag[own_bit, other_bit],
        partner,
    )


def shards(
    amplitudes,
    joined_gates,
    pair_gates,
    global_angles,
    local_phases,
    slice_bits,
    coupled_qubits,
    gate_layout,
):
    row_total = amplitudes.shape[2]
    col_total = amplitudes.shape[3]
    hi_count = lax.axis_size("hi")
    top_bit = lax.axis_size("lo").bit_length() - 2
    source = row_order(gate_layout)
    block = amplitudes
    for layer_id in range(LAYERS):
        angles = qubit_angles(local_phases, slice_bits, coupled_qubits, layer_id)
        row_angles = bit_angles(angles[COL_BITS:], ROW_BITS, ROWS)
        col_angles = bit_angles(angles, COL_BITS, COLS)
        weight_real, weight_imag = folded_gate(
            joined_gates, layer_id, global_angles[layer_id, 0], row_angles
        )
        if layer_id == 0:
            new_real, new_imag = stacked_product(weight_real, weight_imag, block[0, 0], block[1, 0])
        else:
            shaped = block.reshape(2, hi_count, row_total // hi_count, col_total)

            def apply_gate(pieces, weight_real=weight_real, weight_imag=weight_imag):
                item_count = pieces.shape[3]
                flat = pieces.reshape(2, row_total, item_count)
                part_real, part_imag = stacked_product(weight_real, weight_imag, flat[0], flat[1])
                return jnp.stack([part_real, part_imag]).reshape(2, 1, row_total, item_count)

            gated = apply_gate(
                lax.all_to_all(shaped, "hi", split_axis=1, concat_axis=1, tiled=True)
            )
            new_real = gated[0, 0]
            new_imag = gated[1, 0]
        block = column_phase(new_real, new_imag, col_angles)
        block = pair_update(block, pair_gates, layer_id, top_bit if layer_id % 2 == 0 else 0)
        if layer_id + 1 < LAYERS:
            block = jnp.take(block, source, axis=2)
    return block


def solution(mesh):
    placed = (
        P(None, ("hi", "lo"), None, None),
        P(),
        P(),
        P(None, ("hi", "lo")),
        P(),
        P(),
        P(),
        P(),
    )
    return jax.shard_map(
        shards,
        mesh=mesh,
        in_specs=placed,
        out_specs=P(None, ("hi", "lo"), None, None),
        check_vma=False,
    )
```

profile of v0, /device:TPU:5, one launch (start us, length us, event | category | flops | bytes accessed | tf_op | source)
XLA Modules:
  0.0 159.4 jit_solution(9088018951330070262)
XLA Ops:
  0.0 0.8 slice_bitcast_fusion.3
  0.8 0.7 convert_element_type.331
  1.5 0.8 bitcast_add_fusion.5
  2.3 0.7 fusion.33
  3.0 0.7 fusion.35
  3.7 1.4 fusion.34
  5.1 9.8 %fusion.28 = (f32[256]{0:T(256)S(1)}, f32[256]{0:T(256)S(1)}, f32[256]{0:T(256)S(1)}, f32[256]{0:T(256)S(1)}) fusion(f32[]{:T(128)} %bitcast.48, f32[]{:T(128)} %bitcast.47, f32[]{:T(128)} %bitcast.46, f32[]{:T(128)} %bitcast.45, f32[]{:T(128)} %bitcast.44, f32[]{:T(128)} %bitcast.43, f32[]{:T(128)} %bitcast.42, f32[]{:T(128)} %bitcast.41, f32[]{:T(128)} %bitcast.75, ...), kind=kLoop, calls=%fused_computation.101 | loop fusion | flops 13824 | bytes 4160 | tf_op jit(solution)/shard_map/cos | solution.py:70
  14.9 1.3 slice_bitcast_fusion.1
  16.2 6.4 %fusion.24 = (f32[512]{0:T(512)S(1)}, f32[512]{0:T(512)S(1)}) fusion(f32[]{:T(128)} %bitcast.37, f32[]{:T(128)} %bitcast.36, f32[]{:T(128)} %bitcast.35, f32[]{:T(128)} %bitcast.34, f32[]{:T(128)} %bitcast.33, f32[]{:T(128)} %bitcast.32, f32[]{:T(128)} %bitcast.31, f32[]{:T(128)} %bitcast.30, f32[]{:T(128)} %bitcast.29, f32[]{:T(128)} %bitcast.28), kind=kLoop, calls=%fused_computation.97 | loop fusion | flops 23040 | bytes 4136 | tf_op jit(solution)/shard_map/sin | solution.py:41
  22.5 6.4 %fusion.22 = (f32[512]{0:T(512)S(1)}, f32[512]{0:T(512)S(1)}) fusion(f32[]{:T(128)} %bitcast.13, f32[]{:T(128)} %bitcast.12, f32[]{:T(128)} %bitcast.11, f32[]{:T(128)} %bitcast.10, f32[]{:T(128)} %bitcast.9, f32[]{:T(128)} %bitcast.8, f32[]{:T(128)} %bitcast.7, f32[]{:T(128)} %bitcast.6, f32[]{:T(128)} %bitcast.5, f32[]{:T(128)} %bitcast.4), kind=kLoop, calls=%fused_computation.95 | loop fusion | flops 23040 | bytes 4136 | tf_op jit(solution)/shard_map/sin | solution.py:41
  28.9 2.9 %fusion.14 = (f32[512,512]{1,0:T(8,128)S(1)}, f32[512,512]{1,0:T(8,128)S(1)}, f32[512,512]{1,0:T(8,128)S(1)}, f32[512,512]{1,0:T(8,128)S(1)}) fusion(f32[2,2,512,512]{3,2,1,0:T(8,128)} %param.9, f32[512]{0:T(512)S(1)} %get-tuple-element.92, f32[512]{0:T(512)S(1)} %get-tuple-element.93, f32[512]{0:T(512)S(1)} %get-tuple-element.91, f32[512]{0:T(512)S(1)} %get-tuple-element.90), kind=kLoop, calls=%fused_computation.21 | loop fusion | flops 3145728 | bytes 8396800 | tf_op jit(solution)/shard_map/sub | solution.py:44
  31.8 3.4 %fusion.4 = f32[1024,512]{1,0:T(8,128)S(1)} fusion(f32[512,512]{1,0:T(8,128)S(1)} %get-tuple-element.12, f32[512,512]{1,0:T(8,128)S(1)} %get-tuple-element.11, f32[512,256]{1,0:T(8,128)S(1)} %get-tuple-element.28, f32[512,256]{1,0:T(8,128)S(1)} %get-tuple-element.27), kind=kOutput, calls=%fused_computation.5 | convolution fusion | flops 3222011904 | bytes 5242880 | tf_op jit(solution)/shard_map/dot_general | solution.py:61
  35.3 0.2 multiply_add_fusion.1
  35.4 1.0 maximum_bitcast_fusion
  36.5 5.3 %collective-permute-start = (f32[2,1,512,256]{3,2,0,1:T(8,128)}, f32[2,1,512,256]{3,2,0,1:T(8,128)}, u32[]{:S(2)}, u32[]{:S(2)}) collective-permute-start(f32[2,1,512,256]{3,2,0,1:T(8,128)} %maximum_bitcast_fusion), channel_id=1, source_target_pairs={{0,16},{1,17},{2,18},{3,19},{4,20},{5,21},{6,22},{7,23},{8,24},{9,... | collective-permute-start | bytes 3145736 | tf_op jit(solution)/shard_map/ppermute | solution.py:19
  41.8 0.7 fusion.32
  48.1 0.7 constant_dynamic-slice_fusion.2
  48.8 0.7 constant_dynamic-slice_fusion.6
  49.5 40.4 %collective-permute-done = f32[2,1,512,256]{3,2,0,1:T(8,128)} collective-permute-done((f32[2,1,512,256]{3,2,0,1:T(8,128)}, f32[2,1,512,256]{3,2,0,1:T(8,128)}, u32[]{:S(2)}, u32[]{:S(2)}) %collective-permute-start) | collective-permute-done | bytes 1048608 | tf_op jit(solution)/shard_map/ppermute | solution.py:19
  89.9 3.8 %fusion.21 = (f32[1,1,512,256]{3,2,1,0:T(8,128)S(1)}, f32[1,1,512,256]{3,2,1,0:T(8,128)S(1)}) fusion(f32[512,256]{1,0:T(8,128)S(1)} %get-tuple-element.23, f32[512,256]{1,0:T(8,128)S(1)} %get-tuple-element.24, f32[2,1,512,256]{3,2,1,0:T(8,128)} %bitcast.58, f32[2,1,512,256]{3,2,0,1:T(8,128)} %collective-permute-done, f32[]{:T(128)} %bitcast.56, f32[]{:T(128)} %bitcast.50, ...), kind=kLoop, calls=%fused_computation.45 | loop fusion | flops 1835008 | bytes 3148288 | tf_op jit(solution)/shard_map/stack | solution.py:89
  93.8 1.8 %copy.36 = f32[2,512,256]{2,0,1:T(2,128)} copy(f32[2,512,256]{2,1,0:T(8,128)S(1)} %maximum_bitcast_fusion.1) | data formatting | bytes 2097152 | tf_op jit(solution)/shard_map/stack | solution.py:89
  95.6 3.2 %gather_fusion = f32[512,2,256]{2,1,0:T(2,128)S(1)} fusion(f32[2,512,256]{2,0,1:T(2,128)} %copy.36, s32[1024]{0:T(1024)S(1)} %pad_clamp_fusion), kind=kCustom, calls=%fused_computation | custom fusion | bytes 2099200 | tf_op jit(solution)/shard_map/jit(_take)/gather | solution.py:150
  98.9 1.5 broadcast_select_fusion
  100.4 16.2 %all-to-all-start = ((f32[2,32,16,256]{3,0,2,1:T(2,128)}), f32[2,32,16,256]{3,0,2,1:T(2,128)S(1)}, u32[]{:S(2)}, u32[]{:S(2)}) async-start(f32[2,32,16,256]{3,0,2,1:T(2,128)} %broadcast_select_fusion), calls=%async_computation | async-start | bytes 2097152 | tf_op jit(solution)/shard_map/all_to_all | solution.py:143
  116.6 25.9 %all-to-all-done = f32[2,32,16,256]{3,0,2,1:T(2,128)S(1)} async-done(((f32[2,32,16,256]{3,0,2,1:T(2,128)}), f32[2,32,16,256]{3,0,2,1:T(2,128)S(1)}, u32[]{:S(2)}, u32[]{:S(2)}) %all-to-all-start) | async-done | bytes 1048608 | tf_op jit(solution)/shard_map/all_to_all | solution.py:143
  142.5 1.2 fusion.30
  143.7 3.4 %fusion = f32[1024,512]{1,0:T(8,128)S(1)} fusion(f32[512,512]{1,0:T(8,128)S(1)} %get-tuple-element.15, f32[512,512]{1,0:T(8,128)S(1)} %get-tuple-element.16, f32[512,256]{1,0:T(8,128)S(1)} %bitcast.156, f32[512,256]{1,0:T(8,128)S(1)} %bitcast.157), kind=kOutput, calls=%fused_computation.1 | convolution fusion | flops 3222011904 | bytes 5242880 | tf_op jit(solution)/shard_map/dot_general | solution.py:61
  147.2 0.2 multiply_add_fusion
  147.4 6.0 %collective-permute-start.1 = (f32[2,1,512,256]{3,2,0,1:T(8,128)S(1)}, f32[2,1,512,256]{3,2,0,1:T(8,128)S(1)}, u32[]{:S(2)}, u32[]{:S(2)}) collective-permute-start(f32[2,1,512,256]{3,2,0,1:T(8,128)S(1)} %maximum_bitcast_fusion.2), channel_id=1, source_target_pairs={{0,1},{1,0},{2,3},{3,2},{4,5},{5,4},{6,7},{7,6},{8,9},{9,8},{10,11... | collective-permute-start | bytes 3145736 | tf_op jit(solution)/shard_map/ppermute | solution.py:19
  153.4 2.3 %collective-permute-done.1 = f32[2,1,512,256]{3,2,0,1:T(8,128)S(1)} collective-permute-done((f32[2,1,512,256]{3,2,0,1:T(8,128)S(1)}, f32[2,1,512,256]{3,2,0,1:T(8,128)S(1)}, u32[]{:S(2)}, u32[]{:S(2)}) %collective-permute-start.1) | collective-permute-done | bytes 1048608 | tf_op jit(solution)/shard_map/ppermute | solution.py:19
  155.6 2.7 %fusion.19 = (f32[1,1,512,256]{3,2,1,0:T(8,128)S(1)}, f32[1,1,512,256]{3,2,1,0:T(8,128)S(1)}) fusion(f32[512,256]{1,0:T(8,128)S(1)} %get-tuple-element.21, f32[512,256]{1,0:T(8,128)S(1)} %get-tuple-element.22, f32[2,1,512,256]{3,2,1,0:T(8,128)S(1)} %bitcast.158, f32[2,1,512,256]{3,2,0,1:T(8,128)S(1)} %collective-permute-done.1, f32[]{:T(128)} %bitcast.83, ...), kind=kLoop, calls=%fused_computation.40 | loop fusion | flops 1835008 | bytes 3148288 | tf_op jit(solution)/shard_map/sub | solution.py:78
  158.4 1.0 pad_maximum_fusion
  (16 shorter events, 0.6 us)
Async XLA Ops:
  35.2 6.5 %copy-start = (s32[9]{0:T(128)S(1)}, s32[9]{0:T(128)}, u32[]{:S(2)}) copy-start(s32[9]{0:T(128)} %param.15) | copy-start | bytes 112
  35.2 12.9 %copy-start.1 = (f32[2,2,2,2]{3,2,1,0:T(2,128)S(1)}, f32[2,2,2,2]{3,2,1,0:T(2,128)}, u32[]{:S(2)}) copy-start(f32[2,2,2,2]{3,2,1,0:T(2,128)} %param.10) | copy-start | bytes 196
  36.5 53.5 %collective-permute-start = (f32[2,1,512,256]{3,2,0,1:T(8,128)}, f32[2,1,512,256]{3,2,0,1:T(8,128)}, u32[]{:S(2)}, u32[]{:S(2)}) collective-permute-start(f32[2,1,512,256]{3,2,0,1:T(8,128)} %maximum_bitcast_fusion), channel_id=1, source_target_pairs={{0,16},{1,17},{2,18},{3,19},{4,20},{5,21},{6,22},{7,23},{8,24},{9,... | collective-permute-start | bytes 3145736 | tf_op jit(solution)/shard_map/ppermute | solution.py:19
  100.4 42.1 %all-to-all-start = ((f32[2,32,16,256]{3,0,2,1:T(2,128)}), f32[2,32,16,256]{3,0,2,1:T(2,128)S(1)}, u32[]{:S(2)}, u32[]{:S(2)}) async-start(f32[2,32,16,256]{3,0,2,1:T(2,128)} %broadcast_select_fusion), calls=%async_computation | async-start | bytes 2097152 | tf_op jit(solution)/shard_map/all_to_all | solution.py:143
  147.4 8.2 %collective-permute-start.1 = (f32[2,1,512,256]{3,2,0,1:T(8,128)S(1)}, f32[2,1,512,256]{3,2,0,1:T(8,128)S(1)}, u32[]{:S(2)}, u32[]{:S(2)}) collective-permute-start(f32[2,1,512,256]{3,2,0,1:T(8,128)S(1)} %maximum_bitcast_fusion.2), channel_id=1, source_target_pairs={{0,1},{1,0},{2,3},{3,2},{4,5},{5,4},{6,7},{7,6},{8,9},{9,8},{10,11... | collective-permute-start | bytes 3145736 | tf_op jit(solution)/shard_map/ppermute | solution.py:19
where the time goes:
time: 160 us; the launch traced here: 159 us
  waiting for transfers between devices  68.5 us (43%)
  other arithmetic  37.6 us (24%)
  starting transfers between devices  27.4 us (17%)
  local copies, waits for them, and re-layouts  13.3 us (8%)
  matrix products  6.89 us (4%)
  between operations  5.73 us (4%)
    ppermute x2, waiting for transfers between devices, partner_2(): return lax.ppermute(value, axis, pairs)  42.7 us
    all_to_all x1, waiting for transfers between devices, shards(): lax.all_to_all(shaped, 'hi', split_axis=1, concat_axis=1, tiled=True)  25.9 us
    all_to_all x1, starting transfers between devices, shards(): lax.all_to_all(shaped, 'hi', split_axis=1, concat_axis=1, tiled=True)  16.2 us
    sin x2, other arithmetic, folded_gate(): sine = jnp.sin(turned)[None, :]  12.7 us
    ppermute x2, starting transfers between devices, partner_2(): return lax.ppermute(value, axis, pairs)  11.3 us
    cos x1, other arithmetic, column_phase(): cosine = jnp.cos(col_angles)[None, :]  9.78 us
    dot_general x2, matrix products, stacked_product(): jnp.dot(weights, inputs, precision=lax.Precision.HIGHEST, preferred_eleme...  6.89 us
    another operation x3, other arithmetic, combine(): return jnp.stack([new_real, new_imag])  4.94 us
  transfers between devices with their start and end apart: 3, of which 3 were waited for; matrix products, arithmetic and copies ran while one was open for 1% of the time, Pallas kernels for 0%

commit v1 on v0

v1 whole, which is shorter than its diff:
```python
import functools
import math

import jax
import jax.numpy as jnp
from jax import lax
from jax.experimental import pallas as pl
from jax.experimental.pallas import tpu as pltpu
from jax.sharding import PartitionSpec as P

MESH = pl.DeviceIdType.MESH
ROW_BITS = 9
COL_BITS = 8
FIXED = 17
LQ = 17
ROWS = 512
HALF = 128
NH = 32
NL = 32
NY = 8
NZ = 4
U = ROWS // NH
BLK = 128
NB = ROWS // BLK
TOP = NL.bit_length() - 2
X_STRIDE = 4
DY = (1, -1, 2, -2, 3, -3, 4, 0)
OFFSETS = [(dy, (at + k) % NZ) for k in range(NZ) for at, dy in enumerate(DY)]
OFFSETS = [pair for pair in OFFSETS if pair != (0, 0)]


def cmul(ar, ai, br, bi):
    return ar * br - ai * bi, ar * bi + ai * br


def turn(angle):
    return jnp.cos(angle), jnp.sin(angle)


def split(value):
    high = value.astype(jnp.bfloat16)
    return high, (value - high.astype(jnp.float32)).astype(jnp.bfloat16)


def bit_angles(angles, bit_count, positions):
    summed = jnp.zeros(positions.shape, jnp.float32)
    for bit_pos in range(bit_count):
        chosen = ((positions >> bit_pos) & 1).astype(jnp.float32)
        summed = summed + chosen * angles[bit_pos]
    return summed


def kernel(
    phases, bits, coupled, layout, pair, globals_ref, amp_hbm, gates_hbm, out_ref,
    amp, gates, turned, perm, gate0, gate1, own, msg, relay, landed, outbox, inbox, core_msg, core_in,
    high, low, load_sem, leg_send, leg_recv, all_send, all_recv, core_send, core_recv, near, mid, far,
):
    hi = lax.axis_index("hi")
    lo = lax.axis_index("lo")
    y = lax.rem(hi, NY)
    z = lax.div(hi, NY)
    top = (lo >> TOP) & 1
    bit0 = lo & 1
    x_side = (lax.rem(lo + 2 * X_STRIDE, NL), lax.rem(lo + NL - 2 * X_STRIDE, NL))
    twin = lo ^ 1

    def at(dy, dz):
        return lax.rem(z + dz, NZ) * NY + lax.rem(y + dy + NY, NY)

    loads = [
        pltpu.make_async_copy(amp_hbm, amp, load_sem.at[0]),
        pltpu.make_async_copy(gates_hbm.at[0], gates.at[0], load_sem.at[1]),
        pltpu.make_async_copy(gates_hbm.at[1], gates.at[1], load_sem.at[2]),
    ]
    for load in loads:
        load.start()

    def greet(sem, targets):
        for target in targets:
            pl.semaphore_signal(sem, inc=1, device_id=target, device_id_type=MESH)

    entry = pltpu.get_barrier_semaphore()
    neighbours = [(hi, x_side[0]), (hi, x_side[1]), (hi, twin), (at(1, 0), lo), (at(-1, 0), lo)]
    neighbours += [(at(0, dz), lo) for dz in range(1, NZ)]
    greet(entry, neighbours)

    def leg(phase, step, side, k):
        rows = pl.ds(k * BLK, BLK)
        source = (msg, relay)[step].at[phase, side, rows]
        target = (relay, landed)[step].at[phase, side, rows]
        return pltpu.make_async_remote_copy(
            src_ref=source,
            dst_ref=target,
            send_sem=leg_send.at[phase, step, side, k],
            recv_sem=leg_recv.at[phase, step, side, k],
            device_id=(hi, x_side[side]),
            device_id_type=MESH,
        )

    def core_copy(phase, k):
        rows = pl.ds(k * BLK, BLK)
        return pltpu.make_async_remote_copy(
            src_ref=core_msg.at[phase, :, rows],
            dst_ref=core_in.at[phase, :, rows],
            send_sem=core_send.at[phase, k],
            recv_sem=core_recv.at[phase, k],
            device_id=(hi, twin),
            device_id_type=MESH,
        )

    def send_all(phase):
        for dy, dz in OFFSETS:
            t = at(dy, dz)
            pltpu.make_async_remote_copy(
                src_ref=outbox.at[phase, t],
                dst_ref=inbox.at[phase, hi],
                send_sem=all_send.at[phase],
                recv_sem=all_recv.at[phase],
                device_id=(t, lo),
                device_id_type=MESH,
            ).start()
        inbox[phase, hi] = outbox[phase, hi]

    def everyone(phase):
        return pltpu.make_async_remote_copy(
            src_ref=outbox.at[phase, pl.ds(0, NH - 1)],
            dst_ref=inbox.at[phase, pl.ds(0, NH - 1)],
            send_sem=all_send.at[phase],
            recv_sem=all_recv.at[phase],
            device_id=(hi, twin),
            device_id_type=MESH,
        )

    angles = []
    for layer in range(2):
        row = []
        for q in range(LQ):
            count = jnp.int32(0)
            for f in range(FIXED):
                count = count + jnp.where(coupled[layer, f] == q, bits[f], 0)
            row.append(phases[layer, q] + math.pi * count.astype(jnp.float32))
        angles.append(row)
    row_at = lax.broadcasted_iota(jnp.int32, (1, ROWS), 1)
    row_turn = [turn(bit_angles(angles[layer][COL_BITS:], ROW_BITS, row_at)) for layer in range(2)]
    lane = lax.broadcasted_iota(jnp.int32, (1, HALF), 1)
    first_turn = turn(jnp.full((1, HALF), globals_ref[0, 0]))
    second_turn = turn(jnp.full((1, HALF), globals_ref[1, 0]))

    def coeff(layer, target_bit, source_bit):
        where = layer * 8 + target_bit * 2 + source_bit
        return pair[where], pair[where + 4]

    first_own = coeff(0, top, top)
    first_msg = coeff(0, 1 - top, top)
    last_own = []
    last_msg = []
    for phase in range(2):
        place = lane + phase * HALF
        both = cmul(
            *turn(bit_angles(angles[0], COL_BITS, place)),
            *turn(bit_angles(angles[1], COL_BITS, place)),
        )
        both = cmul(*both, *second_turn)
        last_own.append(cmul(*both, *coeff(1, bit0, bit0)))
        last_msg.append(cmul(*both, *coeff(1, 1 - bit0, bit0)))

    loads[0].wait()
    msg_factor = cmul(*first_turn, *first_msg)
    own_factor = cmul(*first_turn, *first_own)
    for k in range(NB):
        rows = pl.ds(k * BLK, BLK)
        real, imag = amp[0, 0, rows, :HALF], amp[1, 0, rows, :HALF]
        msg[0, 0, rows], msg[0, 1, rows] = cmul(real, imag, *msg_factor)
        own[0, 0, rows], own[0, 1, rows] = cmul(real, imag, *own_factor)
    pl.semaphore_wait(entry, len(neighbours))
    for k in range(NB):
        for side in range(2):
            leg(0, 0, side, k).start()
    greet(near, [(at(1, 0), lo), (at(-1, 0), lo)])

    def fill(k, real, imag):
        rows = pl.ds(k * BLK, BLK)
        high[rows, :HALF], low[rows, :HALF] = split(real)
        high[rows, HALF:], low[rows, HALF:] = split(imag)

    for k in range(NB):
        rows = pl.ds(k * BLK, BLK)
        fill(k, *cmul(amp[0, 0, rows, HALF:], amp[1, 0, rows, HALF:], *first_turn))

    def folded(layer, k):
        rows = pl.ds(pl.multiple_of(k * BLK, BLK), BLK)
        real, imag = cmul(gates[layer, 0, rows], gates[layer, 1, rows], *row_turn[layer])
        return split(real) + split(imag)

    loads[1].wait()

    def fold_first(k, carry):
        rows = pl.ds(pl.multiple_of(k * BLK, BLK), BLK)
        parts = folded(0, k)
        for kind, part in enumerate((parts[0], parts[2], parts[1], parts[3])):
            turned[rows, kind * ROWS : (kind + 1) * ROWS] = part
        return carry

    lax.fori_loop(0, NB, fold_first, 0)
    pl.semaphore_wait(near, 2)
    greet(mid, [(at(2, 0), lo), (at(-2, 0), lo)])

    def permute(k, carry):
        place = lax.broadcasted_iota(jnp.int32, (BLK, HALF), 0) + k * BLK
        source = jnp.zeros((BLK, HALF), jnp.int32)
        for bit_pos in range(ROW_BITS):
            source = source + (((place >> bit_pos) & 1) << layout[bit_pos])
        column = lax.broadcasted_iota(jnp.int32, (BLK, HALF), 1)
        for part in range(ROWS // HALF):
            hit = (source == column + part * HALF).astype(jnp.float32)
            perm[:, part * HALF : (part + 1) * HALF] = hit.astype(jnp.bfloat16)
        for kind in range(4):
            moved = jnp.dot(
                perm[...],
                turned[:, kind * ROWS : (kind + 1) * ROWS],
                preferred_element_type=jnp.float32,
            )
            gate0[k, kind * BLK : (kind + 1) * BLK] = moved.astype(jnp.bfloat16)
        return carry

    lax.fori_loop(0, NB, permute, 0)
    pl.semaphore_wait(mid, 2)
    greet(far, [(at(4, 0), lo)])

    def product(gate, k):
        main = jnp.dot(gate[k], high[...], preferred_element_type=jnp.float32)
        rest = jnp.dot(gate[k, : 2 * BLK], low[...], preferred_element_type=jnp.float32)
        real = main[:BLK] + main[2 * BLK : 3 * BLK] + rest[:BLK]
        imag = main[BLK : 2 * BLK] + main[3 * BLK :] + rest[BLK:]
        return real[:, :HALF] - imag[:, HALF:], real[:, HALF:] + imag[:, :HALF]

    def first_layer(phase):
        def block(k, carry):
            real, imag = product(gate0, k)
            spots = pl.ds(k * (BLK // U), BLK // U)
            outbox[phase, spots, 0] = real.reshape(BLK // U, U, HALF)
            outbox[phase, spots, 1] = imag.reshape(BLK // U, U, HALF)
            return carry

        lax.fori_loop(0, NB, block, 0)

    def collect(phase):
        everyone(phase).wait_recv()
        for k in range(NB):
            spots = pl.ds(k * (BLK // U), BLK // U)
            fill(
                k,
                inbox[phase, spots, 0].reshape(BLK, HALF),
                inbox[phase, spots, 1].reshape(BLK, HALF),
            )

    first_layer(1)
    pl.semaphore_wait(far, 1)
    send_all(1)

    loads[2].wait()

    def fold_second(k, carry):
        parts = folded(1, k)
        for kind, part in enumerate((parts[0], parts[2], parts[1], parts[3])):
            gate1[k, kind * BLK : (kind + 1) * BLK] = part
        return carry

    lax.fori_loop(0, NB, fold_second, 0)

    def pass_on(phase):
        for k in range(NB):
            for side in range(2):
                leg(phase, 0, side, k).wait_recv()
                leg(phase, 1, side, k).start()

    pass_on(0)

    collect(1)
    for k in range(NB):
        rows = pl.ds(k * BLK, BLK)
        real, imag = product(gate1, k)
        msg[1, 0, rows], msg[1, 1, rows] = cmul(real, imag, *first_msg)
        own[1, 0, rows], own[1, 1, rows] = cmul(real, imag, *first_own)
        for side in range(2):
            leg(1, 0, side, k).start()

    for k in range(NB):
        rows = pl.ds(k * BLK, BLK)
        for side in range(2):
            leg(0, 1, side, k).wait_recv()
        fill(k, own[0, 0, rows] + landed[0, 0, rows], own[0, 1, rows] + landed[0, 1, rows])
    first_layer(0)
    send_all(0)

    pass_on(1)

    def finish(phase, k, real, imag):
        rows = pl.ds(k * BLK, BLK)
        core_msg[phase, 0, rows], core_msg[phase, 1, rows] = cmul(real, imag, *last_msg[phase])
        core_copy(phase, k).start()
        own[phase, 0, rows], own[phase, 1, rows] = cmul(real, imag, *last_own[phase])

    def write(phase, k):
        rows = pl.ds(k * BLK, BLK)
        columns = slice(phase * HALF, (phase + 1) * HALF)
        core_copy(phase, k).wait_recv()
        for part in range(2):
            out_ref[part, rows, columns] = own[phase, part, rows] + core_in[phase, part, rows]

    collect(0)
    for k in range(NB):
        finish(0, k, *product(gate1, k))
    for k in range(NB):
        write(0, k)

    for k in range(NB):
        rows = pl.ds(k * BLK, BLK)
        for side in range(2):
            leg(1, 1, side, k).wait_recv()
        finish(1, k, own[1, 0, rows] + landed[1, 0, rows], own[1, 1, rows] + landed[1, 1, rows])
    for k in range(NB):
        write(1, k)

    for phase in range(2):
        everyone(phase).wait_send()
        for k in range(NB):
            core_copy(phase, k).wait_send()
            for step in range(2):
                for side in range(2):
                    leg(phase, step, side, k).wait_send()


def shards(
    amplitudes, joined_gates, pair_gates, global_angles, local_phases, slice_bits, coupled_qubits, gate_layout
):
    smem = pl.BlockSpec(memory_space=pltpu.SMEM)
    hbm = pl.BlockSpec(memory_space=pl.ANY)
    f32, bf16, dma = jnp.float32, jnp.bfloat16, pltpu.SemaphoreType.DMA
    half = pltpu.VMEM((2, 2, ROWS, HALF), f32)
    box = pltpu.VMEM((2, NH, 2, U, HALF), f32)
    out = pl.pallas_call(
        kernel,
        out_shape=jax.ShapeDtypeStruct((2, ROWS, 2 * HALF), f32),
        in_specs=[smem] * 6 + [hbm] * 2,
        out_specs=pl.BlockSpec(memory_space=pltpu.VMEM),
        scratch_shapes=[
            pltpu.VMEM((2, 1, ROWS, 2 * HALF), f32),
            pltpu.VMEM((2, 2, ROWS, ROWS), f32),
            pltpu.VMEM((ROWS, 4 * ROWS), bf16),
            pltpu.VMEM((BLK, ROWS), bf16),
            pltpu.VMEM((NB, 4 * BLK, ROWS), bf16),
            pltpu.VMEM((NB, 4 * BLK, ROWS), bf16),
            half, half, half, half, box, box, half, half,
            pltpu.VMEM((ROWS, 2 * HALF), bf16),
            pltpu.VMEM((ROWS, 2 * HALF), bf16),
            dma((3,)), dma((2, 2, 2, NB)), dma((2, 2, 2, NB)), dma((2,)), dma((2,)), dma((2, NB)), dma((2, NB)),
            pltpu.SemaphoreType.REGULAR, pltpu.SemaphoreType.REGULAR, pltpu.SemaphoreType.REGULAR,
        ],
        compiler_params=pltpu.CompilerParams(
            collective_id=0, has_side_effects=True, vmem_limit_bytes=56 << 20
        ),
        name="two_layers",
    )(
        local_phases, slice_bits, coupled_qubits, gate_layout, pair_gates.reshape(-1), global_angles,
        amplitudes, joined_gates,
    )
    return out[:, None]


def solution(mesh):
    placed = (
        P(None, ("hi", "lo"), None, None),
        P(),
        P(),
        P(None, ("hi", "lo")),
        P(),
        P(),
        P(),
        P(),
    )
    return jax.shard_map(
        shards,
        mesh=mesh,
        in_specs=placed,
        out_specs=P(None, ("hi", "lo"), None, None),
        check_vma=False,
    )
```

time: 160 us -> 72.9 us (0.46)
  the two profiles are of different devices: /device:TPU:5 before, /device:TPU:1 now
where the time goes in v1:
time: 72.9 us; the launch traced here: 72.7 us
  Pallas kernels  67.8 us (93%)
  local copies, waits for them, and re-layouts  4.92 us (7%)
    pallas_call x1, Pallas kernels, shards(): pl.pallas_call(kernel, out_shape=jax.ShapeDtypeStruct((2, ROWS, 2 * HALF)...  67.8 us
    unnamed x2, local copies, waits for them, and re-layouts  3.56 us

profile of v1, /device:TPU:1, one launch (start us, length us, event | category | flops | bytes accessed | tf_op | source)
XLA Modules:
  0.0 72.7 jit_solution(2369202745616515065)
XLA Ops:
  0.0 1.4 %reshape.3.pair = f32[16]{0:T(128)} reshape(f32[2,2,2,2]{3,2,1,0:T(2,128)} %param.10) | data formatting | bytes 128 | tf_op jit(solution)/shard_map/reshape | solution.py:365
  1.4 1.3 %copy.9.globals_ref = f32[2,1]{1,0:T(2,128)} copy(f32[2,1]{0,1:T(1,128)} %param.11) | data formatting | bytes 16 | tf_op args[3]
  2.7 67.8 %two_layers.1 = f32[2,512,256]{2,1,0:T(8,128)} custom-call(f32[2,17]{1,0:T(2,128)} %phases.1, s32[17]{0:T(128)} %bits.1, s32[2,17]{1,0:T(2,128)} %coupled.1, s32[9]{0:T(128)} %layout.1, f32[16]{0:T(128)} %reshape.3.pair, f32[2,1]{1,0:T(2,128)} %copy.9.globals_ref, f32[2,1,512,256]{3,2,1,0:T(8,128)} %amp_hbm.1, f32[2,2,512,512]{3,2,1,0:T(8,128)} %gates_hbm.1), custom_call_target="tpu_custom_call" | custom-call | tf_op jit(solution)/shard_map/two_layers/pallas_call | solution.py:342
  70.4 2.3 %copy.12 = f32[2,1,512,256]{3,2,1,0:T(8,128)} copy(f32[2,1,512,256]{3,2,1,0:T(8,128)} %bitcast.3) | data formatting | bytes 2097152

commit v2 on v1

--- a/solution.py
+++ b/solution.py
@@ -24,6 +24,8 @@
 NB = ROWS // BLK
 TOP = NL.bit_length() - 2
 X_STRIDE = 4
+STEPS = 4
+HOP = 4 // STEPS
 DY = (1, -1, 2, -2, 3, -3, 4, 0)
 OFFSETS = [(dy, (at + k) % NZ) for k in range(NZ) for at, dy in enumerate(DY)]
 OFFSETS = [pair for pair in OFFSETS if pair != (0, 0)]
@@ -52,8 +54,8 @@
 
 def kernel(
     phases, bits, coupled, layout, pair, globals_ref, amp_hbm, gates_hbm, out_ref,
-    amp, gates, turned, perm, gate0, gate1, own, msg, relay, landed, outbox, inbox, core_msg, core_in,
-    high, low, load_sem, leg_send, leg_recv, all_send, all_recv, core_send, core_recv, near, mid, far,
+    amp, gates, perm, gate0, gate1, own, msg, relay, landed, outbox, inbox, core_msg, core_in,
+    high, low, made_high, made_low, load_sem, leg_send, leg_recv, all_send, all_recv, core_send, core_recv, near, mid, far,
 ):
     hi = lax.axis_index("hi")
     lo = lax.axis_index("lo")
@@ -61,7 +63,7 @@
     z = lax.div(hi, NY)
     top = (lo >> TOP) & 1
     bit0 = lo & 1
-    x_side = (lax.rem(lo + 2 * X_STRIDE, NL), lax.rem(lo + NL - 2 * X_STRIDE, NL))
+    x_side = (lax.rem(lo + HOP * X_STRIDE, NL), lax.rem(lo + NL - HOP * X_STRIDE, NL))
     twin = lo ^ 1
 
     def at(dy, dz):
@@ -86,8 +88,9 @@
 
     def leg(phase, step, side, k):
         rows = pl.ds(k * BLK, BLK)
-        source = (msg, relay)[step].at[phase, side, rows]
-        target = (relay, landed)[step].at[phase, side, rows]
+        places = [msg, *(relay.at[at_step] for at_step in range(STEPS - 1)), landed]
+        source = places[step].at[phase, side, rows]
+        target = places[step + 1].at[phase, side, rows]
         return pltpu.make_async_remote_copy(
             src_ref=source,
             dst_ref=target,
@@ -131,38 +134,29 @@
             device_id_type=MESH,
         )
 
-    angles = []
-    for layer in range(2):
+    def qubit_angles(layer):
         row = []
         for q in range(LQ):
             count = jnp.int32(0)
             for f in range(FIXED):
                 count = count + jnp.where(coupled[layer, f] == q, bits[f], 0)
             row.append(phases[layer, q] + math.pi * count.astype(jnp.float32))
-        angles.append(row)
-    row_at = lax.broadcasted_iota(jnp.int32, (1, ROWS), 1)
-    row_turn = [turn(bit_angles(angles[layer][COL_BITS:], ROW_BITS, row_at)) for layer in range(2)]
-    lane = lax.broadcasted_iota(jnp.int32, (1, HALF), 1)
+        return row
+
+    def row_turn(angles):
+        return turn(bit_angles(angles[COL_BITS:], ROW_BITS, lax.broadcasted_iota(jnp.int32, (1, ROWS), 1)))
+
+    def coeff(layer, target_bit, source_bit):
+        return pair[layer, 0, target_bit, source_bit], pair[layer, 1, target_bit, source_bit]
+
     first_turn = turn(jnp.full((1, HALF), globals_ref[0, 0]))
-    second_turn = turn(jnp.full((1, HALF), globals_ref[1, 0]))
-
-    def coeff(layer, target_bit, source_bit):
-        where = layer * 8 + target_bit * 2 + source_bit
-        return pair[where], pair[where + 4]
-
     first_own = coeff(0, top, top)
     first_msg = coeff(0, 1 - top, top)
-    last_own = []
-    last_msg = []
-    for phase in range(2):
-        place = lane + phase * HALF
-        both = cmul(
-            *turn(bit_angles(angles[0], COL_BITS, place)),
-            *turn(bit_angles(angles[1], COL_BITS, place)),
-        )
-        both = cmul(*both, *second_turn)
-        last_own.append(cmul(*both, *coeff(1, bit0, bit0)))
-        last_msg.append(cmul(*both, *coeff(1, 1 - bit0, bit0)))
+
+    def fill(k, real, imag):
+        rows = pl.ds(k * BLK, BLK)
+        high[rows, :HALF], low[rows, :HALF] = split(real)
+        high[rows, HALF:], low[rows, HALF:] = split(imag)
 
     loads[0].wait()
     msg_factor = cmul(*first_turn, *first_msg)
@@ -171,41 +165,36 @@
         rows = pl.ds(k * BLK, BLK)
         real, imag = amp[0, 0, rows, :HALF], amp[1, 0, rows, :HALF]
         msg[0, 0, rows], msg[0, 1, rows] = cmul(real, imag, *msg_factor)
-        own[0, 0, rows], own[0, 1, rows] = cmul(real, imag, *own_factor)
     pl.semaphore_wait(entry, len(neighbours))
     for k in range(NB):
         for side in range(2):
             leg(0, 0, side, k).start()
     greet(near, [(at(1, 0), lo), (at(-1, 0), lo)])
 
-    def fill(k, real, imag):
-        rows = pl.ds(k * BLK, BLK)
-        high[rows, :HALF], low[rows, :HALF] = split(real)
-        high[rows, HALF:], low[rows, HALF:] = split(imag)
-
     for k in range(NB):
         rows = pl.ds(k * BLK, BLK)
         fill(k, *cmul(amp[0, 0, rows, HALF:], amp[1, 0, rows, HALF:], *first_turn))
 
-    def folded(layer, k):
-        rows = pl.ds(pl.multiple_of(k * BLK, BLK), BLK)
-        real, imag = cmul(gates[layer, 0, rows], gates[layer, 1, rows], *row_turn[layer])
-        return split(real) + split(imag)
+    first_angles = qubit_angles(0)
+    turned = row_turn(first_angles)
+
+    def fold(layer, gate, factors):
+        def block(k, carry):
+            rows = pl.ds(pl.multiple_of(k * BLK, BLK), BLK)
+            real, imag = cmul(gates[layer, 0, rows], gates[layer, 1, rows], *factors)
+            parts = split(real) + split(imag)
+            for kind, part in enumerate((parts[0], parts[2], parts[1], parts[3])):
+                gate[k, kind * BLK : (kind + 1) * BLK] = part
+            return carry
+
+        lax.fori_loop(0, NB, block, 0)
 
     loads[1].wait()
-
-    def fold_first(k, carry):
-        rows = pl.ds(pl.multiple_of(k * BLK, BLK), BLK)
-        parts = folded(0, k)
-        for kind, part in enumerate((parts[0], parts[2], parts[1], parts[3])):
-            turned[rows, kind * ROWS : (kind + 1) * ROWS] = part
-        return carry
-
-    lax.fori_loop(0, NB, fold_first, 0)
+    fold(0, gate0, turned)
     pl.semaphore_wait(near, 2)
     greet(mid, [(at(2, 0), lo), (at(-2, 0), lo)])
 
-    def permute(k, carry):
+    def order(k, carry):
         place = lax.broadcasted_iota(jnp.int32, (BLK, HALF), 0) + k * BLK
         source = jnp.zeros((BLK, HALF), jnp.int32)
         for bit_pos in range(ROW_BITS):
@@ -213,19 +202,10 @@
         column = lax.broadcasted_iota(jnp.int32, (BLK, HALF), 1)
         for part in range(ROWS // HALF):
             hit = (source == column + part * HALF).astype(jnp.float32)
-            perm[:, part * HALF : (part + 1) * HALF] = hit.astype(jnp.bfloat16)
-        for kind in range(4):
-            moved = jnp.dot(
-                perm[...],
-                turned[:, kind * ROWS : (kind + 1) * ROWS],
-                preferred_element_type=jnp.float32,
-            )
-            gate0[k, kind * BLK : (kind + 1) * BLK] = moved.astype(jnp.bfloat16)
+            perm[k, :, part * HALF : (part + 1) * HALF] = hit.astype(jnp.bfloat16)
         return carry
 
-    lax.fori_loop(0, NB, permute, 0)
-    pl.semaphore_wait(mid, 2)
-    greet(far, [(at(4, 0), lo)])
+    lax.fori_loop(0, NB, order, 0)
 
     def product(gate, k):
         main = jnp.dot(gate[k], high[...], preferred_element_type=jnp.float32)
@@ -234,12 +214,23 @@
         imag = main[BLK : 2 * BLK] + main[3 * BLK :] + rest[BLK:]
         return real[:, :HALF] - imag[:, HALF:], real[:, HALF:] + imag[:, :HALF]
 
-    def first_layer(phase):
+    def first_products():
         def block(k, carry):
+            rows = pl.ds(pl.multiple_of(k * BLK, BLK), BLK)
             real, imag = product(gate0, k)
+            made_high[rows, :HALF], made_low[rows, :HALF] = split(real)
+            made_high[rows, HALF:], made_low[rows, HALF:] = split(imag)
+            return carry
+
+        lax.fori_loop(0, NB, block, 0)
+
+    def reorder(phase):
+        def block(k, carry):
+            moved = jnp.dot(perm[k], made_high[...], preferred_element_type=jnp.float32)
+            moved = moved + jnp.dot(perm[k], made_low[...], preferred_element_type=jnp.float32)
             spots = pl.ds(k * (BLK // U), BLK // U)
-            outbox[phase, spots, 0] = real.reshape(BLK // U, U, HALF)
-            outbox[phase, spots, 1] = imag.reshape(BLK // U, U, HALF)
+            outbox[phase, spots, 0] = moved[:, :HALF].reshape(BLK // U, U, HALF)
+            outbox[phase, spots, 1] = moved[:, HALF:].reshape(BLK // U, U, HALF)
             return carry
 
         lax.fori_loop(0, NB, block, 0)
@@ -254,27 +245,45 @@
                 inbox[phase, spots, 1].reshape(BLK, HALF),
             )
 
-    first_layer(1)
+    first_products()
+    pl.semaphore_wait(mid, 2)
+    greet(far, [(at(4, 0), lo)])
+    reorder(1)
     pl.semaphore_wait(far, 1)
     send_all(1)
 
+    def pass_on(phase, step, k):
+        for side in range(2):
+            leg(phase, step - 1, side, k).wait_recv()
+            leg(phase, step, side, k).start()
+
+    for k in range(NB):
+        pass_on(0, 1, k)
+
+    for k in range(NB):
+        rows = pl.ds(k * BLK, BLK)
+        real, imag = amp[0, 0, rows, :HALF], amp[1, 0, rows, :HALF]
+        own[0, 0, rows], own[0, 1, rows] = cmul(real, imag, *own_factor)
+    second_angles = qubit_angles(1)
     loads[2].wait()
-
-    def fold_second(k, carry):
-        parts = folded(1, k)
-        for kind, part in enumerate((parts[0], parts[2], parts[1], parts[3])):
-            gate1[k, kind * BLK : (kind + 1) * BLK] = part
-        return carry
-
-    lax.fori_loop(0, NB, fold_second, 0)
-
-    def pass_on(phase):
+    fold(1, gate1, row_turn(second_angles))
+    lane = lax.broadcasted_iota(jnp.int32, (1, HALF), 1)
+    second_turn = turn(jnp.full((1, HALF), globals_ref[0, 1]))
+    last_own = []
+    last_msg = []
+    for phase in range(2):
+        place = lane + phase * HALF
+        both = cmul(
+            *turn(bit_angles(first_angles, COL_BITS, place)),
+            *turn(bit_angles(second_angles, COL_BITS, place)),
+        )
+        both = cmul(*both, *second_turn)
+        last_own.append(cmul(*both, *coeff(1, bit0, bit0)))
+        last_msg.append(cmul(*both, *coeff(1, 1 - bit0, bit0)))
+
+    for step in range(2, STEPS):
         for k in range(NB):
-            for side in range(2):
-                leg(phase, 0, side, k).wait_recv()
-                leg(phase, 1, side, k).start()
-
-    pass_on(0)
+            pass_on(0, step, k)
 
     collect(1)
     for k in range(NB):
@@ -288,12 +297,15 @@
     for k in range(NB):
         rows = pl.ds(k * BLK, BLK)
         for side in range(2):
-            leg(0, 1, side, k).wait_recv()
+            leg(0, STEPS - 1, side, k).wait_recv()
         fill(k, own[0, 0, rows] + landed[0, 0, rows], own[0, 1, rows] + landed[0, 1, rows])
-    first_layer(0)
+    first_products()
+    reorder(0)
     send_all(0)
 
-    pass_on(1)
+    for step in range(1, STEPS - 1):
+        for k in range(NB):
+            pass_on(1, step, k)
 
     def finish(phase, k, real, imag):
         rows = pl.ds(k * BLK, BLK)
@@ -311,13 +323,14 @@
     collect(0)
     for k in range(NB):
         finish(0, k, *product(gate1, k))
+        pass_on(1, STEPS - 1, k)
     for k in range(NB):
         write(0, k)
 
     for k in range(NB):
         rows = pl.ds(k * BLK, BLK)
         for side in range(2):
-            leg(1, 1, side, k).wait_recv()
+            leg(1, STEPS - 1, side, k).wait_recv()
         finish(1, k, own[1, 0, rows] + landed[1, 0, rows], own[1, 1, rows] + landed[1, 1, rows])
     for k in range(NB):
         write(1, k)
@@ -326,7 +339,7 @@
         everyone(phase).wait_send()
         for k in range(NB):
             core_copy(phase, k).wait_send()
-            for step in range(2):
+            for step in range(STEPS):
                 for side in range(2):
                     leg(phase, step, side, k).wait_send()
 
@@ -335,7 +348,7 @@
     amplitudes, joined_gates, pair_gates, global_angles, local_phases, slice_bits, coupled_qubits, gate_layout
 ):
     smem = pl.BlockSpec(memory_space=pltpu.SMEM)
-    hbm = pl.BlockSpec(memory_space=pl.ANY)
+    hbm = pl.BlockSpec(memory_space=pltpu.HBM)
     f32, bf16, dma = jnp.float32, jnp.bfloat16, pltpu.SemaphoreType.DMA
     half = pltpu.VMEM((2, 2, ROWS, HALF), f32)
     box = pltpu.VMEM((2, NH, 2, U, HALF), f32)
@@ -347,22 +360,20 @@
         scratch_shapes=[
             pltpu.VMEM((2, 1, ROWS, 2 * HALF), f32),
             pltpu.VMEM((2, 2, ROWS, ROWS), f32),
-            pltpu.VMEM((ROWS, 4 * ROWS), bf16),
-            pltpu.VMEM((BLK, ROWS), bf16),
+            pltpu.VMEM((NB, BLK, ROWS), bf16),
             pltpu.VMEM((NB, 4 * BLK, ROWS), bf16),
             pltpu.VMEM((NB, 4 * BLK, ROWS), bf16),
-            half, half, half, half, box, box, half, half,
-            pltpu.VMEM((ROWS, 2 * HALF), bf16),
-            pltpu.VMEM((ROWS, 2 * HALF), bf16),
-            dma((3,)), dma((2, 2, 2, NB)), dma((2, 2, 2, NB)), dma((2,)), dma((2,)), dma((2, NB)), dma((2, NB)),
+            half, half, pltpu.VMEM((STEPS - 1, 2, 2, ROWS, HALF), f32), half, box, box, half, half,
+            *[pltpu.VMEM((ROWS, 2 * HALF), bf16)] * 4,
+            dma((3,)), dma((2, STEPS, 2, NB)), dma((2, STEPS, 2, NB)), dma((2,)), dma((2,)), dma((2, NB)), dma((2, NB)),
             pltpu.SemaphoreType.REGULAR, pltpu.SemaphoreType.REGULAR, pltpu.SemaphoreType.REGULAR,
         ],
         compiler_params=pltpu.CompilerParams(
-            collective_id=0, has_side_effects=True, vmem_limit_bytes=56 << 20
+            collective_id=0, has_side_effects=True, vmem_limit_bytes=58 << 20
         ),
         name="two_layers",
     )(
-        local_phases, slice_bits, coupled_qubits, gate_layout, pair_gates.reshape(-1), global_angles,
+        local_phases, slice_bits, coupled_qubits, gate_layout, pair_gates, global_angles.T,
         amplitudes, joined_gates,
     )
     return out[:, None]

time: 72.9 us -> 70.1 us (0.962)
  local copies, waits for them, and re-layouts: 4.92 us -> 2.26 us
    reshape x1 -> x0, local copies, waits for them, and re-layouts: 1.36 us -> none  [shards(): pair_gates.reshape(-1)]
    unnamed x2 -> x1, local copies, waits for them, and re-layouts: 3.56 us -> 2.26 us
where the time goes in v2:
time: 70.1 us; the launch traced here: 69.9 us
  Pallas kernels  67.7 us (97%)
  local copies, waits for them, and re-layouts  2.26 us (3%)
    pallas_call x1, Pallas kernels, shards(): pl.pallas_call(kernel, out_shape=jax.ShapeDtypeStruct((2, ROWS, 2 * HALF)...  67.7 us
    unnamed x1, local copies, waits for them, and re-layouts  2.26 us

profile of v2, /device:TPU:1, one launch (start us, length us, event | category | flops | bytes accessed | tf_op | source)
XLA Modules:
  0.0 69.9 jit_solution(5761238500470380876)
XLA Ops:
  0.0 67.7 %two_layers.1 = f32[2,512,256]{2,1,0:T(8,128)} custom-call(f32[2,17]{1,0:T(2,128)} %phases.1, s32[17]{0:T(128)} %bits.1, s32[2,17]{1,0:T(2,128)} %coupled.1, s32[9]{0:T(128)} %layout.1, f32[2,2,2,2]{3,2,1,0:T(2,128)} %pair.1, f32[1,2]{1,0:T(1,128)} %bitcast.5, f32[2,1,512,256]{3,2,1,0:T(8,128)} %amp_hbm.1, f32[2,2,512,512]{3,2,1,0:T(8,128)} %gates_hbm.1), custom_call_target="tpu_custom_call" | custom-call | tf_op jit(solution)/shard_map/two_layers/pallas_call | solution.py:355
  67.7 2.3 %copy.11 = f32[2,1,512,256]{3,2,1,0:T(8,128)} copy(f32[2,1,512,256]{3,2,1,0:T(8,128)} %bitcast.4) | data formatting | bytes 2097152

commit v3 on v2

--- a/solution.py
+++ b/solution.py
@@ -74,7 +74,7 @@
         pltpu.make_async_copy(gates_hbm.at[0], gates.at[0], load_sem.at[1]),
         pltpu.make_async_copy(gates_hbm.at[1], gates.at[1], load_sem.at[2]),
     ]
-    for load in loads:
+    for load in loads[:2]:
         load.start()
 
     def greet(sem, targets):
@@ -158,42 +158,6 @@
         high[rows, :HALF], low[rows, :HALF] = split(real)
         high[rows, HALF:], low[rows, HALF:] = split(imag)
 
-    loads[0].wait()
-    msg_factor = cmul(*first_turn, *first_msg)
-    own_factor = cmul(*first_turn, *first_own)
-    for k in range(NB):
-        rows = pl.ds(k * BLK, BLK)
-        real, imag = amp[0, 0, rows, :HALF], amp[1, 0, rows, :HALF]
-        msg[0, 0, rows], msg[0, 1, rows] = cmul(real, imag, *msg_factor)
-    pl.semaphore_wait(entry, len(neighbours))
-    for k in range(NB):
-        for side in range(2):
-            leg(0, 0, side, k).start()
-    greet(near, [(at(1, 0), lo), (at(-1, 0), lo)])
-
-    for k in range(NB):
-        rows = pl.ds(k * BLK, BLK)
-        fill(k, *cmul(amp[0, 0, rows, HALF:], amp[1, 0, rows, HALF:], *first_turn))
-
-    first_angles = qubit_angles(0)
-    turned = row_turn(first_angles)
-
-    def fold(layer, gate, factors):
-        def block(k, carry):
-            rows = pl.ds(pl.multiple_of(k * BLK, BLK), BLK)
-            real, imag = cmul(gates[layer, 0, rows], gates[layer, 1, rows], *factors)
-            parts = split(real) + split(imag)
-            for kind, part in enumerate((parts[0], parts[2], parts[1], parts[3])):
-                gate[k, kind * BLK : (kind + 1) * BLK] = part
-            return carry
-
-        lax.fori_loop(0, NB, block, 0)
-
-    loads[1].wait()
-    fold(0, gate0, turned)
-    pl.semaphore_wait(near, 2)
-    greet(mid, [(at(2, 0), lo), (at(-2, 0), lo)])
-
     def order(k, carry):
         place = lax.broadcasted_iota(jnp.int32, (BLK, HALF), 0) + k * BLK
         source = jnp.zeros((BLK, HALF), jnp.int32)
@@ -206,6 +170,43 @@
         return carry
 
     lax.fori_loop(0, NB, order, 0)
+
+    first_angles = qubit_angles(0)
+    turned = row_turn(first_angles)
+
+    loads[0].wait()
+    msg_factor = cmul(*first_turn, *first_msg)
+    own_factor = cmul(*first_turn, *first_own)
+    for k in range(NB):
+        rows = pl.ds(k * BLK, BLK)
+        real, imag = amp[0, 0, rows, :HALF], amp[1, 0, rows, :HALF]
+        msg[0, 0, rows], msg[0, 1, rows] = cmul(real, imag, *msg_factor)
+    pl.semaphore_wait(entry, len(neighbours))
+    for k in range(NB):
+        for side in range(2):
+            leg(0, 0, side, k).start()
+    greet(near, [(at(1, 0), lo), (at(-1, 0), lo)])
+
+    for k in range(NB):
+        rows = pl.ds(k * BLK, BLK)
+        fill(k, *cmul(amp[0, 0, rows, HALF:], amp[1, 0, rows, HALF:], *first_turn))
+
+    def fold(layer, gate, factors):
+        def block(k, carry):
+            rows = pl.ds(pl.multiple_of(k * BLK, BLK), BLK)
+            real, imag = cmul(gates[layer, 0, rows], gates[layer, 1, rows], *factors)
+            parts = split(real) + split(imag)
+            for kind, part in enumerate((parts[0], parts[2], parts[1], parts[3])):
+                gate[k, kind * BLK : (kind + 1) * BLK] = part
+            return carry
+
+        lax.fori_loop(0, NB, block, 0)
+
+    loads[1].wait()
+    loads[2].start()
+    fold(0, gate0, turned)
+    pl.semaphore_wait(near, 2)
+    greet(mid, [(at(2, 0), lo), (at(-2, 0), lo)])
 
     def product(gate, k):
         main = jnp.dot(gate[k], high[...], preferred_element_type=jnp.float32)
@@ -303,7 +304,7 @@
     reorder(0)
     send_all(0)
 
-    for step in range(1, STEPS - 1):
+    for step in range(1, STEPS):
         for k in range(NB):
             pass_on(1, step, k)
 
@@ -323,7 +324,6 @@
     collect(0)
     for k in range(NB):
         finish(0, k, *product(gate1, k))
-        pass_on(1, STEPS - 1, k)
     for k in range(NB):
         write(0, k)
 
@@ -369,12 +369,17 @@
             pltpu.SemaphoreType.REGULAR, pltpu.SemaphoreType.REGULAR, pltpu.SemaphoreType.REGULAR,
         ],
         compiler_params=pltpu.CompilerParams(
-            collective_id=0, has_side_effects=True, vmem_limit_bytes=58 << 20
+            collective_id=0, has_side_effects=True, vmem_limit_bytes=40 << 20
         ),
         name="two_layers",
     )(
-        local_phases, slice_bits, coupled_qubits, gate_layout, pair_gates, global_angles.T,
-        amplitudes, joined_gates,
+        *(
+            pltpu.with_memory_space_constraint(array, pltpu.HBM)
+            for array in (
+                local_phases, slice_bits, coupled_qubits, gate_layout, pair_gates, global_angles.T,
+                amplitudes, joined_gates,
+            )
+        ),
     )
     return out[:, None]
 

time: 70.1 us -> 67.1 us (0.957)
  Pallas kernels: 67.7 us -> 66 us
  local copies, waits for them, and re-layouts: 2.26 us -> 0.97 us
    pallas_call x1, Pallas kernels: 67.7 us -> 66 us  [shards(): pl.pallas_call(kernel, out_shape=jax.ShapeDtypeStruct((2, ROWS, 2 * HALF)...]
    unnamed x1, local copies, waits for them, and re-layouts: 2.26 us -> 0.97 us
where the time goes in v3:
time: 67.1 us; the launch traced here: 66.9 us
  Pallas kernels  66 us (98%)
  local copies, waits for them, and re-layouts  0.97 us (1%)
    pallas_call x1, Pallas kernels, shards(): pl.pallas_call(kernel, out_shape=jax.ShapeDtypeStruct((2, ROWS, 2 * HALF)...  66 us

profile of v3, /device:TPU:1, one launch (start us, length us, event | category | flops | bytes accessed | tf_op | source)
XLA Modules:
  0.0 66.9 jit_solution(465923860672308436)
XLA Ops:
  0.0 66.0 %two_layers.1 = f32[2,512,256]{2,1,0:T(8,128)S(1)} custom-call(f32[2,17]{1,0:T(2,128)} %phases.1, s32[17]{0:T(128)} %bits.1, s32[2,17]{1,0:T(2,128)} %coupled.1, s32[9]{0:T(128)} %layout.1, f32[2,2,2,2]{3,2,1,0:T(2,128)} %pair.1, f32[1,2]{1,0:T(1,128)} %bitcast.5, f32[2,1,512,256]{3,2,1,0:T(8,128)} %amp_hbm.1, f32[2,2,512,512]{3,2,1,0:T(8,128)} %gates_hbm.1), custom_call_target="tpu_custom_call" | custom-call | tf_op jit(solution)/shard_map/two_layers/pallas_call | solution.py:355
  66.0 1.0 %copy.11 = f32[2,1,512,256]{3,2,1,0:T(8,128)} copy(f32[2,1,512,256]{3,2,1,0:T(8,128)S(1)} %bitcast.4) | data formatting | bytes 2097152

commit v4 on v3

--- a/solution.py
+++ b/solution.py
@@ -26,6 +26,9 @@
 X_STRIDE = 4
 STEPS = 4
 HOP = 4 // STEPS
+RELAYS = sorted(
+    ((step, k) for step in range(1, STEPS) for k in range(NB)), key=lambda item: (item[1] + 2 * item[0], item[0])
+)
 DY = (1, -1, 2, -2, 3, -3, 4, 0)
 OFFSETS = [(dy, (at + k) % NZ) for k in range(NZ) for at, dy in enumerate(DY)]
 OFFSETS = [pair for pair in OFFSETS if pair != (0, 0)]
@@ -258,8 +261,8 @@
             leg(phase, step - 1, side, k).wait_recv()
             leg(phase, step, side, k).start()
 
-    for k in range(NB):
-        pass_on(0, 1, k)
+    for step, k in RELAYS[:3]:
+        pass_on(0, step, k)
 
     for k in range(NB):
         rows = pl.ds(k * BLK, BLK)
@@ -282,9 +285,8 @@
         last_own.append(cmul(*both, *coeff(1, bit0, bit0)))
         last_msg.append(cmul(*both, *coeff(1, 1 - bit0, bit0)))
 
-    for step in range(2, STEPS):
-        for k in range(NB):
-            pass_on(0, step, k)
+    for step, k in RELAYS[3:]:
+        pass_on(0, step, k)
 
     collect(1)
     for k in range(NB):
@@ -304,9 +306,8 @@
     reorder(0)
     send_all(0)
 
-    for step in range(1, STEPS):
-        for k in range(NB):
-            pass_on(1, step, k)
+    for step, k in RELAYS:
+        pass_on(1, step, k)
 
     def finish(phase, k, real, imag):
         rows = pl.ds(k * BLK, BLK)

time: 67.1 us -> 67.9 us (1.012)
  Pallas kernels: 66 us -> 66.8 us
    pallas_call x1, Pallas kernels: 66 us -> 66.8 us  [shards(): pl.pallas_call(kernel, out_shape=jax.ShapeDtypeStruct((2, ROWS, 2 * HALF)...]
where the time goes in v4:
time: 67.9 us; the launch traced here: 67.7 us
  Pallas kernels  66.8 us (98%)
  local copies, waits for them, and re-layouts  0.97 us (1%)
    pallas_call x1, Pallas kernels, shards(): pl.pallas_call(kernel, out_shape=jax.ShapeDtypeStruct((2, ROWS, 2 * HALF)...  66.8 us

profile of v4, /device:TPU:1, one launch (start us, length us, event | category | flops | bytes accessed | tf_op | source)
XLA Modules:
  0.0 67.7 jit_solution(1073863886644152403)
XLA Ops:
  0.0 66.8 %two_layers.1 = f32[2,512,256]{2,1,0:T(8,128)S(1)} custom-call(f32[2,17]{1,0:T(2,128)} %phases.1, s32[17]{0:T(128)} %bits.1, s32[2,17]{1,0:T(2,128)} %coupled.1, s32[9]{0:T(128)} %layout.1, f32[2,2,2,2]{3,2,1,0:T(2,128)} %pair.1, f32[1,2]{1,0:T(1,128)} %bitcast.5, f32[2,1,512,256]{3,2,1,0:T(8,128)} %amp_hbm.1, f32[2,2,512,512]{3,2,1,0:T(8,128)} %gates_hbm.1), custom_call_target="tpu_custom_call" | custom-call | tf_op jit(solution)/shard_map/two_layers/pallas_call | solution.py:356
  66.8 1.0 %copy.11 = f32[2,1,512,256]{3,2,1,0:T(8,128)} copy(f32[2,1,512,256]{3,2,1,0:T(8,128)S(1)} %bitcast.4) | data formatting | bytes 2097152

commit v5 on v3

--- a/solution.py
+++ b/solution.py
@@ -158,6 +158,19 @@
         high[rows, :HALF], low[rows, :HALF] = split(real)
         high[rows, HALF:], low[rows, HALF:] = split(imag)
 
+    loads[0].wait()
+    msg_factor = cmul(*first_turn, *first_msg)
+    own_factor = cmul(*first_turn, *first_own)
+    for k in range(NB):
+        rows = pl.ds(k * BLK, BLK)
+        real, imag = amp[0, 0, rows, :HALF], amp[1, 0, rows, :HALF]
+        msg[0, 0, rows], msg[0, 1, rows] = cmul(real, imag, *msg_factor)
+    pl.semaphore_wait(entry, len(neighbours))
+    for k in range(NB):
+        for side in range(2):
+            leg(0, 0, side, k).start()
+    greet(near, [(at(1, 0), lo), (at(-1, 0), lo)])
+
     def order(k, carry):
         place = lax.broadcasted_iota(jnp.int32, (BLK, HALF), 0) + k * BLK
         source = jnp.zeros((BLK, HALF), jnp.int32)
@@ -173,19 +186,6 @@
 
     first_angles = qubit_angles(0)
     turned = row_turn(first_angles)
-
-    loads[0].wait()
-    msg_factor = cmul(*first_turn, *first_msg)
-    own_factor = cmul(*first_turn, *first_own)
-    for k in range(NB):
-        rows = pl.ds(k * BLK, BLK)
-        real, imag = amp[0, 0, rows, :HALF], amp[1, 0, rows, :HALF]
-        msg[0, 0, rows], msg[0, 1, rows] = cmul(real, imag, *msg_factor)
-    pl.semaphore_wait(entry, len(neighbours))
-    for k in range(NB):
-        for side in range(2):
-            leg(0, 0, side, k).start()
-    greet(near, [(at(1, 0), lo), (at(-1, 0), lo)])
 
     for k in range(NB):
         rows = pl.ds(k * BLK, BLK)

time: 67.1 us -> 67.2 us (level)
  no operation moved by 1% of the time
where the time goes in v5:
time: 67.2 us; the launch traced here: 67 us
  Pallas kernels  66.1 us (98%)
  local copies, waits for them, and re-layouts  0.97 us (1%)
    pallas_call x1, Pallas kernels, shards(): pl.pallas_call(kernel, out_shape=jax.ShapeDtypeStruct((2, ROWS, 2 * HALF)...  66.1 us

profile of v5, /device:TPU:1, one launch (start us, length us, event | category | flops | bytes accessed | tf_op | source)
XLA Modules:
  0.0 67.0 jit_solution(16709041799230633723)
XLA Ops:
  0.0 66.1 %two_layers.1 = f32[2,512,256]{2,1,0:T(8,128)S(1)} custom-call(f32[2,17]{1,0:T(2,128)} %phases.1, s32[17]{0:T(128)} %bits.1, s32[2,17]{1,0:T(2,128)} %coupled.1, s32[9]{0:T(128)} %layout.1, f32[2,2,2,2]{3,2,1,0:T(2,128)} %pair.1, f32[1,2]{1,0:T(1,128)} %bitcast.5, f32[2,1,512,256]{3,2,1,0:T(8,128)} %amp_hbm.1, f32[2,2,512,512]{3,2,1,0:T(8,128)} %gates_hbm.1), custom_call_target="tpu_custom_call" | custom-call | tf_op jit(solution)/shard_map/two_layers/pallas_call | solution.py:355
  66.1 1.0 %copy.11 = f32[2,1,512,256]{3,2,1,0:T(8,128)} copy(f32[2,1,512,256]{3,2,1,0:T(8,128)S(1)} %bitcast.4) | data formatting | bytes 2097152
